TPU v7x, 512 devices: a whole 4x8x8 slice. The times are simulated.
512 devices in a mesh: tp: 8 (over z), ep: 64 (over y, x, core).
Axes of the slice: x: 4, y: 8, z: 8, core: 2. Of those that a mesh axis runs over, the one named last changes fastest.
Arguments:
- attn: bfloat16 [32768, 1536], P('ep', 'tp'), may hold values from -6 to 6
- resid: bfloat16 [32768, 1536], P('ep', 'tp'), may hold values from -6 to 6
- w_out: bfloat16 [1536, 1536], P('tp', 'ep'), may hold values from -0.15625 to 0.15625
- gain_mix: float32 [1536], replicated, may hold values from 0.1 to 1.9
- gain_out: float32 [1536], replicated, may hold values from 0.1 to 1.9
- routes: int32 [32768, 8], P('ep'), may hold values from 0 to 39, all different within a row; in each aligned block of 64 rows (0 to 63, 64 to 127, ...) at most 16 rows name the same one
- gates: float32 [32768, 8], P('ep'), may hold values from 0.05 to 1
- w_gate: bfloat16 [64, 1536, 512], P('ep'), as said below
- w_up: bfloat16 [64, 1536, 512], P('ep'), as said below
- w_down: bfloat16 [64, 512, 1536], P('ep'), as said below
Outputs:
- layer_out: bfloat16 [32768, 1536], P('ep', 'tp')
Inputs may be any that keep to these rules, and one draw needn't show every extreme that they name: `routes`: in each aligned block of 64 rows no expert is named more than 16 times; each row names 8 different experts. `w_gate`: copy s holds the weights of expert s % 40. `w_up`: copy s holds the weights of expert s % 40. `w_down`: copy s holds the weights of expert s % 40.
All inputs are finite; a program needn't handle non-finite values.
Results may differ from a plain program's by a relative error of at most 0.0053.
Values may be sent and summed in bfloat16 or wider, within the bound.
No kernel may reach another device: no remote copies, remote signals or barrier semaphores. Data moves between devices by JAX's collectives and lax.ppermute only.
A program may use at most 64 MiB of HBM per device.

v0:
```python
import jax
import jax.numpy as jnp
from jax import lax
from jax.experimental import pallas as pl
from jax.experimental.pallas import tpu as pltpu
from jax.sharding import Mesh, PartitionSpec as P

EXPERTS = 40
CAP = 16
EPS = 1e-05
BF = jnp.bfloat16
F32 = jnp.float32
EP = ("h", "y", "x", "c")
VMEM = 56 * 1024 * 1024


def params():
    return pltpu.CompilerParams(vmem_limit_bytes=VMEM)


def dot(a, b, ca, cb):
    return lax.dot_general(a, b, (((ca,), (cb,)), ((), ())), preferred_element_type=F32)


def pack_kernel(attn_ref, resid_ref, w_ref, out_ref):
    both = jnp.concatenate([attn_ref[...], resid_ref[...]], axis=0)
    turned = both.T
    out_ref[:, 0:64, :] = turned.reshape(8, 64, 384)
    for i in range(8):
        out_ref[i, 64:88, 192:384] = jnp.zeros((24, 192), BF)
        out_ref[i, 64:88, 0:192] = w_ref[...]


def unpack_kernel(got_ref, routes_ref, tok_ref, w_ref):
    for z in range(8):
        at = z * 192
        tok_ref[:, at : at + 192] = got_ref[z, 0:64, 0:192]
        tok_ref[:, 1536 + at : 1728 + at] = got_ref[z, 0:64, 192:384]
        for y in range(8):
            w_ref[y, :, at : at + 192] = got_ref[z, 64:88, 0:192]
    tok_ref[:, 3072:3200] = jnp.zeros((64, 128), BF)
    tok_ref[:, 3072:3080] = routes_ref[...].astype(F32).astype(BF)


def piece_kernel(place_ref, wg_ref, wu_ref, wd_ref, out_ref):
    out_ref[0:192, :] = wg_ref[0]
    out_ref[192:384, :] = wu_ref[0]
    for i in range(3):
        out_ref[384 + i * 64 : 448 + i * 64, :] = wd_ref[0, :, i * 512 : (i + 1) * 512]


def one_hot_rows(routed, expert, rank_of):
    hits = jnp.zeros((routed.shape[0], expert.shape[1]), F32)
    for k in range(8):
        hits = hits + jnp.where(routed[:, k : k + 1] == expert, 1.0, 0.0)
    ranks = dot(rank_of, hits.astype(BF), 1, 0)
    return hits, ranks


def before_matrix(rows):
    a = lax.broadcasted_iota(jnp.int32, (rows, rows), 0)
    b = lax.broadcasted_iota(jnp.int32, (rows, rows), 1)
    keep = (b < a) & (a // 64 == b // 64)
    return jnp.where(keep, 1.0, 0.0).astype(BF)


def mix_kernel(place_ref, tok_ref, wa_ref, wb_ref, gain_ref, send_ref, hid_ref, w_scr, h_scr, n_scr):
    core, row, local = place_ref[0], place_ref[1], place_ref[2]
    for ref, off in ((wa_ref, core * 24), (wb_ref, (1 - core) * 24)):
        for y in range(8):
            for x in range(4):
                at = pl.multiple_of((y * 4 + x) * 48 + off, 8)
                w_scr[pl.ds(at, 24), :] = ref[x, y * 24 : (y + 1) * 24, :]
    total = jnp.zeros((256, 1), F32)
    attn = tok_ref[:, 0:1536]
    for n in range(0, 1536, 256):
        part = dot(attn, w_scr[n : n + 256, :], 1, 1) + tok_ref[:, 1536 + n : 1792 + n].astype(F32)
        h_scr[:, n : n + 256] = part
        total = total + jnp.sum(part * part, axis=1, keepdims=True)
    scale = lax.rsqrt(total / 1536 + EPS)
    n_scr[...] = (h_scr[...] * scale * gain_ref[...]).astype(BF)

    lane = lax.broadcasted_iota(jnp.int32, (1, 128), 1)
    slot = lane // CAP
    want = (lane % CAP).astype(F32)
    near = ((8 * row + slot) % EXPERTS).astype(F32)
    far = (jnp.where(row < 4, 32, 24) + slot).astype(F32)
    routed = tok_ref[:, 3072:3200].astype(F32)
    hits, ranks = one_hot_rows(routed, near, before_matrix(256))
    pick = jnp.where(ranks == want, hits, 0.0).astype(BF)
    for b in range(4):
        rows = dot(pick[b * 64 : (b + 1) * 64], n_scr[b * 64 : (b + 1) * 64, :], 0, 0)
        send_ref[:, b * CAP : (b + 1) * CAP, :] = rows.astype(BF).reshape(8, CAP, 1536)
    mine = pl.ds(pl.multiple_of(local * 64, 64), 64)
    hits, ranks = one_hot_rows(tok_ref[mine, 3072:3200].astype(F32), far, before_matrix(64))
    pick = jnp.where(ranks == want, hits, 0.0).astype(BF)
    rows = dot(pick, n_scr[mine, :], 0, 0)
    send_ref[:, 64:80, :] = rows.astype(BF).reshape(8, CAP, 1536)
    hid_ref[...] = h_scr[mine, :]


def expert(x, w_gate, w_up, w_down):
    gate = dot(x, w_gate, 1, 0)
    up = dot(x, w_up, 1, 0)
    act = (gate / (1.0 + jnp.exp(-gate)) * up).astype(BF)
    return dot(act, w_down, 1, 0).astype(BF)


def near_kernel(x_ref, wg_ref, wu_ref, wd_ref, out_ref):
    x = jnp.concatenate([x_ref[:, i * CAP : (i + 1) * CAP, :].reshape(128, 1536) for i in range(2)], axis=0)
    y = expert(x, wg_ref[0], wu_ref[0], wd_ref[0])
    out_ref[...] = y.reshape(2, 8, CAP, 1536)


def far_kernel(place_ref, x_ref, w_ref, *refs):
    out_refs, (wg_scr, wu_scr, wd_scr, y_scr) = refs[0:8], refs[8:]
    me = place_ref[5]
    for z in range(8):
        wg_scr[z * 192 : (z + 1) * 192, :] = w_ref[z, 0:192, :]
        wu_scr[z * 192 : (z + 1) * 192, :] = w_ref[z, 192:384, :]
        for i in range(3):
            wd_scr[z * 64 : (z + 1) * 64, i * 512 : (i + 1) * 512] = w_ref[z, 384 + i * 64 : 448 + i * 64, :]
    y_scr[...] = expert(x_ref[...].reshape(128, 1536), wg_scr[...], wu_scr[...], wd_scr[...])
    for k in range(8):
        out_refs[k][...] = y_scr[pl.ds(pl.multiple_of((me + k) % 8 * CAP, CAP), CAP), :]


def close_kernel(place_ref, routes_ref, gates_ref, hid_ref, gain_ref, near_ref, *refs):
    far_refs, out_ref = refs[0:8], refs[8]
    lane = lax.broadcasted_iota(jnp.int32, (1, 640), 1)
    half, me, slot = place_ref[3], place_ref[5], lane // CAP
    near_of, far_of = (32 * half + slot) % EXPERTS, 32 - 8 * half + (me + 40 - slot) % 8
    expert_of = jnp.where(slot < 32, near_of, far_of).astype(F32)
    routed = routes_ref[...].astype(F32)
    hits, ranks = one_hot_rows(routed, expert_of, before_matrix(64))
    gate = jnp.zeros((64, 640), F32)
    for k in range(8):
        gate = gate + jnp.where(routed[:, k : k + 1] == expert_of, gates_ref[:, k : k + 1], 0.0)
    gate = jnp.where((ranks == (lane % CAP).astype(F32)) & (hits > 0.5), gate, 0.0)
    high = gate.astype(BF)
    low = (gate - high.astype(F32)).astype(BF)
    both = jnp.concatenate([high, low], axis=0)
    far = jnp.concatenate([ref[...] for ref in far_refs], axis=0)
    total = dot(both[:, 0:512], near_ref[...].reshape(512, 1536), 1, 0) + dot(both[:, 512:640], far, 1, 0)
    combined = hid_ref[...] + (total[0:64] + total[64:128])
    mean = jnp.sum(combined * combined, axis=1, keepdims=True) / 1536
    out = (combined * lax.rsqrt(mean + EPS) * gain_ref[...]).astype(BF)
    for z in range(8):
        out_ref[z] = out[:, z * 192 : (z + 1) * 192]


def smem():
    return pl.BlockSpec(memory_space=pltpu.SMEM)


def vmem():
    return pl.BlockSpec(memory_space=pltpu.VMEM)


def keep(value):
    return pltpu.with_memory_space_constraint(value, pltpu.VMEM)


def per_device(attn, resid, w_out, gain_mix, gain_out, routes, gates, w_gate, w_up, w_down):
    tp, h, y = lax.axis_index("tp"), lax.axis_index("h"), lax.axis_index("y")
    core, me = lax.axis_index("c"), lax.axis_index(("x", "c"))
    place = jnp.stack([core, h * 4 + y, y, h, tp, me])
    shape = jax.ShapeDtypeStruct
    my_routes = lax.dynamic_slice_in_dim(routes, tp * 64, 64, 0)
    my_gates = lax.dynamic_slice_in_dim(gates, tp * 64, 64, 0)

    send = pl.pallas_call(
        pack_kernel,
        out_shape=shape((8, 88, 384), BF),
        in_specs=[vmem()] * 3,
        out_specs=vmem(),
        compiler_params=params(),
        name="pack",
    )(attn.T, resid.T, w_out.T)
    got = lax.all_to_all(send, "tp", 0, 0, tiled=True)

    piece = pl.pallas_call(
        piece_kernel,
        grid_spec=pltpu.PrefetchScalarGridSpec(
            num_scalar_prefetch=1,
            grid=(1,),
            in_specs=[
                pl.BlockSpec((1, 192, 512), lambda i, p: (0, p[4], 0)),
                pl.BlockSpec((1, 192, 512), lambda i, p: (0, p[4], 0)),
                pl.BlockSpec((1, 64, 1536), lambda i, p: (0, p[4], 0)),
            ],
            out_specs=pl.BlockSpec((576, 512), lambda i, p: (0, 0)),
        ),
        out_shape=shape((576, 512), BF),
        compiler_params=params(),
        name="piece",
    )(place, w_gate, w_up, w_down)
    across = lambda v, a, b, c, d: lax.ppermute(v, ("h", "y"), [(a, b), (c, d)])
    step_1 = across(piece, 4, 3, 3, 4)
    step_3 = across(piece, 4, 1, 3, 6)
    got, step_1 = lax.optimization_barrier((got, step_1))

    tokens, w_y = pl.pallas_call(
        unpack_kernel,
        out_shape=(shape((64, 3200), BF), shape((8, 24, 1536), BF)),
        in_specs=[vmem()] * 2,
        out_specs=(vmem(), vmem()),
        compiler_params=params(),
        name="unpack",
    )(keep(got), my_routes)
    tokens, w_y, step_3 = lax.optimization_barrier((tokens, w_y, step_3))
    tokens = lax.all_gather(tokens, "y", axis=0, tiled=True)
    w_y = lax.all_to_all(w_y, ("h", "y"), 0, 0, tiled=True)
    w_x = lax.all_to_all(jnp.broadcast_to(w_y.reshape(1, 192, 1536), (4, 192, 1536)), "x", 0, 0, tiled=True)
    w_x, tokens, step_1, step_3 = lax.optimization_barrier((w_x, tokens, step_1, step_3))
    w_c = lax.ppermute(w_x, "c", [(0, 1), (1, 0)])
    step_2 = across(step_1, 3, 2, 4, 5)
    step_4 = across(step_3, 1, 0, 6, 7)

    send, hidden = pl.pallas_call(
        mix_kernel,
        out_shape=(shape((8, 80, 1536), BF), shape((64, 1536), F32)),
        in_specs=[smem()] + [vmem()] * 4,
        out_specs=(vmem(), vmem()),
        scratch_shapes=[pltpu.VMEM((1536, 1536), BF), pltpu.VMEM((256, 1536), F32), pltpu.VMEM((256, 1536), BF)],
        compiler_params=params(),
        name="mix",
    )(place, tokens, w_x, w_c, gain_mix.reshape(1, 1536))
    step_2, step_4, _ = lax.optimization_barrier((step_2, step_4, send))
    far_piece = (step_1 + step_2) + (step_3 + step_4)
    far_weights = lax.all_gather(far_piece, "tp", axis=0, tiled=False)
    received = lax.all_to_all(send, ("x", "c"), 0, 0, tiled=True)

    whole = lambda *dims: pl.BlockSpec(dims, lambda i: (0,) * len(dims))
    near = pl.pallas_call(
        near_kernel,
        grid=(2,),
        out_shape=shape((4, 8, CAP, 1536), BF),
        in_specs=[
            pl.BlockSpec((8, 2 * CAP, 1536), lambda i: (0, i, 0)),
            whole(1, 1536, 512),
            whole(1, 1536, 512),
            whole(1, 512, 1536),
        ],
        out_specs=pl.BlockSpec((2, 8, CAP, 1536), lambda i: (i, 0, 0, 0)),
        compiler_params=params(),
        name="near",
    )(received, w_gate, w_up, w_down)
    near = lax.all_to_all(near.reshape(32, CAP, 1536), ("y", "x", "c"), 0, 0, tiled=True)
    far = pl.pallas_call(
        far_kernel,
        grid=(1,),
        out_shape=(shape((CAP, 1536), BF),) * 8,
        in_specs=[smem(), pl.BlockSpec((8, CAP, 1536), lambda i: (0, 4, 0))] + [whole(8, 576, 512)],
        out_specs=(whole(CAP, 1536),) * 8,
        scratch_shapes=[
            pltpu.VMEM((1536, 512), BF),
            pltpu.VMEM((1536, 512), BF),
            pltpu.VMEM((512, 1536), BF),
            pltpu.VMEM((128, 1536), BF),
        ],
        compiler_params=params(),
        name="far",
    )(place, received, far_weights)
    far = [far[0]] + [lax.ppermute(far[k], ("x", "c"), [(i, (i + k) % 8) for i in range(8)]) for k in range(1, 8)]

    finished = pl.pallas_call(
        close_kernel,
        out_shape=shape((8, 64, 192), BF),
        in_specs=[smem()] + [vmem()] * 13,
        out_specs=vmem(),
        compiler_params=params(),
        name="close",
    )(place, my_routes, my_gates, hidden, gain_out.reshape(1, 1536), keep(near), *far)
    return lax.all_to_all(finished, "tp", 0, 0, tiled=True).reshape(512, 192)


def solution(mesh):
    fine = Mesh(mesh.devices.reshape(8, 2, 4, 4, 2), ("tp",) + EP)
    return jax.shard_map(
        per_device,
        mesh=fine,
        in_specs=(
            P(EP, "tp"),
            P(EP, "tp"),
            P("tp", EP),
            P(),
            P(),
            P(EP, None),
            P(EP, None),
            P(EP, None, None),
            P(EP, None, None),
            P(EP, None, None),
        ),
        out_specs=P(EP, "tp"),
        check_vma=False,
    )
```

profile of v0, /device:TPU:57, one launch (start us, length us, event | category | flops | bytes accessed | tf_op | source)
XLA Modules:
  0.0 246.7 jit_solution(3379368323104836097)
XLA Ops:
  6.5 2.0 pack.1
  8.6 10.0 %all-to-all-start = ((bf16[8,88,384]{2,1,0:T(8,128)(2,1)}), bf16[8,88,384]{2,1,0:T(8,128)(2,1)S(1)}, u32[]{:S(2)}, u32[]{:S(2)}) async-start(bf16[8,88,384]{2,1,0:T(8,128)(2,1)} %pack.1), calls=%async_computation | async-start | bytes 1081344 | tf_op jit(solution)/shard_map/all_to_all | solution.py:180
  19.2 2.7 %piece.1 = bf16[576,512]{1,0:T(8,128)(2,1)} custom-call(s32[6]{0:T(128)} %stack.27.place_ref, bf16[1,1536,512]{2,1,0:T(8,128)(2,1)} %wg_ref.3, bf16[1,1536,512]{2,1,0:T(8,128)(2,1)} %wu_ref.3, bf16[1,512,1536]{2,1,0:T(8,128)(2,1)} %wd_ref.3), custom_call_target="tpu_custom_call" | custom-call | tf_op jit(solution)/shard_map/piece/pallas_call | solution.py:182
  24.1 12.8 %all-to-all-done.got_ref = bf16[8,88,384]{2,1,0:T(8,128)(2,1)S(1)} async-done(((bf16[8,88,384]{2,1,0:T(8,128)(2,1)}), bf16[8,88,384]{2,1,0:T(8,128)(2,1)S(1)}, u32[]{:S(2)}, u32[]{:S(2)}) %all-to-all-start) | async-done | bytes 540704 | tf_op jit(solution)/shard_map/all_to_all | solution.py:180
  36.9 2.0 unpack.1
  38.9 19.1 %all-to-all-start.1 = ((bf16[8,24,1536]{2,1,0:T(8,128)(2,1)}), bf16[8,24,1536]{2,1,0:T(8,128)(2,1)S(1)}, u32[]{:S(2)}, u32[]{:S(2)}) async-start(bf16[8,24,1536]{2,1,0:T(8,128)(2,1)} %get-tuple-element.31), calls=%async_computation.1 | async-start | bytes 1179648 | tf_op jit(solution)/shard_map/all_to_all | solution.py:213
  58.7 9.5 %all-to-all-done.1 = bf16[8,24,1536]{2,1,0:T(8,128)(2,1)S(1)} async-done(((bf16[8,24,1536]{2,1,0:T(8,128)(2,1)}), bf16[8,24,1536]{2,1,0:T(8,128)(2,1)S(1)}, u32[]{:S(2)}, u32[]{:S(2)}) %all-to-all-start.1) | async-done | bytes 589856 | tf_op jit(solution)/shard_map/all_to_all | solution.py:213
  69.9 4.0 %all-to-all-start.2 = ((bf16[4,192,1536]{2,1,0:T(8,128)(2,1)}), bf16[4,192,1536]{2,1,0:T(8,128)(2,1)S(1)}, u32[]{:S(2)}, u32[]{:S(2)}) async-start(bf16[4,192,1536]{2,1,0:T(8,128)(2,1)} %broadcast_in_dim.8), calls=%async_computation.2 | async-start | bytes 4718592 | tf_op jit(solution)/shard_map/all_to_all | solution.py:214
  73.9 35.8 %all-gather.4.cloned.1.call-done.tok_ref = bf16[256,3200]{1,0:T(8,128)(2,1)} async-done(((bf16[64,3200]{1,0:T(8,128)(2,1)}), bf16[256,3200]{1,0:T(8,128)(2,1)}) %all-gather.4.cloned.1.call-update) | async-done | bytes 1638416 | tf_op jit(solution)/shard_map/all_gather | solution.py:212
  109.7 2.6 %collective-permute-start.2 = (bf16[4,192,1536]{2,1,0:T(8,128)(2,1)S(1)}, bf16[4,192,1536]{2,1,0:T(8,128)(2,1)S(1)}, u32[]{:S(2)}, u32[]{:S(2)}) collective-permute-start(bf16[4,192,1536]{2,1,0:T(8,128)(2,1)S(1)} %all-to-all-done.2.wa_ref), channel_id=1, source_target_pairs={{0,1},{1,0},{2,3},{3,2},{4,5},{5,4},{6,7},{7,6},{8,9},{9,8},{10,11... | collective-permute-start | bytes 7077896 | tf_op jit(solution)/shard_map/ppermute | solution.py:216
  117.9 6.9 %mix.1 = (bf16[8,80,1536]{2,1,0:T(8,128)(2,1)}, f32[64,1536]{1,0:T(8,128)}) custom-call(s32[6]{0:T(128)} %stack.27.place_ref, bf16[256,3200]{1,0:T(8,128)(2,1)} %all-gather.4.cloned.1.call-done.tok_ref, bf16[4,192,1536]{2,1,0:T(8,128)(2,1)} %copy-done.1, bf16[4,192,1536]{2,1,0:T(8,128)(2,1)} %copy-done.2, f32[1,1536]{1,0:T(1,128)} %reshape.14.gain_ref), custom_call_target="tpu_custom_call" | custom-call | tf_op jit(solution)/shard_map/mix/pallas_call | solution.py:220
  124.8 5.1 %collective-permute-done.4 = bf16[576,512]{1,0:T(8,128)(2,1)S(1)} collective-permute-done((bf16[576,512]{1,0:T(8,128)(2,1)S(1)}, bf16[576,512]{1,0:T(8,128)(2,1)S(1)}, u32[]{:S(2)}, u32[]{:S(2)}) %collective-permute-start.4) | collective-permute-done | bytes 589856 | tf_op jit(solution)/shard_map/ppermute | solution.py:198
  130.9 30.2 %all_to_all.30.x_ref = bf16[8,80,1536]{2,1,0:T(8,128)(2,1)} all-to-all(bf16[8,80,1536]{2,1,0:T(8,128)(2,1)S(1)} %copy-done.3), channel_id=1, replica_groups=mesh['tp'=8,'h'=2,'y'=4,'x'=4,'c'=2] {'x','c'}, dimensions={0} | all-to-all | bytes 3932160 | tf_op jit(solution)/shard_map/all_to_all | solution.py:232
  161.0 6.6 %near.1 = bf16[4,8,16,1536]{3,2,1,0:T(8,128)(2,1)} custom-call(bf16[8,80,1536]{2,1,0:T(8,128)(2,1)} %all_to_all.30.x_ref, bf16[1,1536,512]{2,1,0:T(8,128)(2,1)} %wg_ref.3, bf16[1,1536,512]{2,1,0:T(8,128)(2,1)} %wu_ref.3, bf16[1,512,1536]{2,1,0:T(8,128)(2,1)} %wd_ref.3), custom_call_target="tpu_custom_call" | custom-call | tf_op jit(solution)/shard_map/near/pallas_call | solution.py:235
  167.6 6.4 %all-to-all-start.4 = ((bf16[32,16,1536]{2,1,0:T(8,128)(2,1)}), bf16[32,16,1536]{2,1,0:T(8,128)(2,1)S(1)}, u32[]{:S(2)}, u32[]{:S(2)}) async-start(bf16[32,16,1536]{2,1,0:T(8,128)(2,1)} %bitcast.13), calls=%async_computation.4 | async-start | bytes 3145728 | tf_op jit(solution)/shard_map/all_to_all | solution.py:249
  174.0 19.0 %all-gather.6.cloned.1.call-done = bf16[4608,512]{1,0:T(8,128)(2,1)} async-done(((bf16[576,512]{1,0:T(8,128)(2,1)}), bf16[4608,512]{1,0:T(8,128)(2,1)}) %all-gather.6.cloned.1.call-update) | async-done | bytes 4718608 | tf_op jit(solution)/shard_map/all_gather | solution.py:231
  193.0 4.1 %far.1 = (bf16[16,1536]{1,0:T(8,128)(2,1)}, bf16[16,1536]{1,0:T(8,128)(2,1)}, bf16[16,1536]{1,0:T(8,128)(2,1)}, bf16[16,1536]{1,0:T(8,128)(2,1)}, bf16[16,1536]{...) custom-call(s32[6]{0:T(128)} %stack.27.place_ref, ...), custom_call_target="tpu_custom_call" | custom-call | tf_op jit(solution)/shard_map/far/pallas_call | solution.py:250
  197.1 4.3 %collective-permute-start.10 = (bf16[16,1536]{1,0:T(8,128)(2,1)}, bf16[16,1536]{1,0:T(8,128)(2,1)S(1)}, u32[]{:S(2)}, u32[]{:S(2)}) collective-permute-start(bf16[16,1536]{1,0:T(8,128)(2,1)} %get-tuple-element.49), channel_id=1, source_target_pairs={{0,6},{1,7},{2,0},{3,1},{4,2},{5,3},{6,4},{7,5},{8,14},{9,15},{10,... | collective-permute-start | bytes 147464 | tf_op jit(solution)/shard_map/ppermute | solution.py:265
  203.2 1.9 collective-permute-start.6
  205.1 3.5 %collective-permute-start.7 = (bf16[16,1536]{1,0:T(8,128)(2,1)}, bf16[16,1536]{1,0:T(8,128)(2,1)S(1)}, u32[]{:S(2)}, u32[]{:S(2)}) collective-permute-start(bf16[16,1536]{1,0:T(8,128)(2,1)} %get-tuple-element.46), channel_id=1, source_target_pairs={{0,3},{1,4},{2,5},{3,6},{4,7},{5,0},{6,1},{7,2},{8,11},{9,12},{10,... | collective-permute-start | bytes 147464 | tf_op jit(solution)/shard_map/ppermute | solution.py:265
  208.7 3.5 %collective-permute-start.8 = (bf16[16,1536]{1,0:T(8,128)(2,1)}, bf16[16,1536]{1,0:T(8,128)(2,1)S(1)}, u32[]{:S(2)}, u32[]{:S(2)}) collective-permute-start(bf16[16,1536]{1,0:T(8,128)(2,1)} %get-tuple-element.47), channel_id=1, source_target_pairs={{0,4},{1,5},{2,6},{3,7},{4,0},{5,1},{6,2},{7,3},{8,12},{9,13},{10,... | collective-permute-start | bytes 147464 | tf_op jit(solution)/shard_map/ppermute | solution.py:265
  212.2 4.3 %collective-permute-start.9 = (bf16[16,1536]{1,0:T(8,128)(2,1)}, bf16[16,1536]{1,0:T(8,128)(2,1)S(1)}, u32[]{:S(2)}, u32[]{:S(2)}) collective-permute-start(bf16[16,1536]{1,0:T(8,128)(2,1)} %get-tuple-element.48), channel_id=1, source_target_pairs={{0,5},{1,6},{2,7},{3,0},{4,1},{5,2},{6,3},{7,4},{8,13},{9,14},{10,... | collective-permute-start | bytes 147464 | tf_op jit(solution)/shard_map/ppermute | solution.py:265
  220.0 2.9 %close.1 = bf16[8,64,192]{2,1,0:T(8,128)(2,1)} custom-call(s32[6]{0:T(128)} %stack.27.place_ref, s32[64,8]{1,0:T(8,128)} %copy.14.routes_ref, f32[64,8]{1,0:T(8,128)} %copy.15.gates_ref, f32[64,1536]{1,0:T(8,128)} %get-tuple-element.37.hid_ref, f32[1,1536]{1,0:T(1,128)} %reshape.15.gain_ref, bf16[32,16,1536]{2,1,0:T(8,128)(2,1)S(1)} %all-to-all-done.4.near_ref, ...), custom_call_target="tpu_custom_call" | custom-call | tf_op jit(solution)/shard_map/close/pallas_call | solution.py:267
  222.8 16.2 %all_to_all.31 = bf16[8,64,192]{2,1,0:T(8,128)(2,1)S(1)} all-to-all(bf16[8,64,192]{2,1,0:T(8,128)(2,1)} %close.1), channel_id=1, replica_groups=mesh['tp'=8,'h'=2,'y'=4,'x'=4,'c'=2] {'tp'}, dimensions={0} | all-to-all | bytes 393216 | tf_op jit(solution)/shard_map/all_to_all | solution.py:275
  (57 shorter events, 17.7 us)
Async XLA Ops:
  6.5 16.8 %copy-start = (s32[512,8]{0,1:T(8,128)S(1)}, s32[512,8]{0,1:T(8,128)}, u32[]{:S(2)}) copy-start(s32[512,8]{0,1:T(8,128)} %param.15) | copy-start | bytes 49156
  8.6 28.3 %all-to-all-start = ((bf16[8,88,384]{2,1,0:T(8,128)(2,1)}), bf16[8,88,384]{2,1,0:T(8,128)(2,1)S(1)}, u32[]{:S(2)}, u32[]{:S(2)}) async-start(bf16[8,88,384]{2,1,0:T(8,128)(2,1)} %pack.1), calls=%async_computation | async-start | bytes 1081344 | tf_op jit(solution)/shard_map/all_to_all | solution.py:180
  21.9 2.2 collective-permute-start
  22.6 16.3 %collective-permute-start.1 = (bf16[576,512]{1,0:T(8,128)(2,1)}, bf16[576,512]{1,0:T(8,128)(2,1)S(1)}, u32[]{:S(2)}, u32[]{:S(2)}) collective-permute-start(bf16[576,512]{1,0:T(8,128)(2,1)} %piece.1), channel_id=1, source_target_pairs={{32,8},{24,48},{33,9},{25,49},{34,10},{26,50},{35,11},{27,51},{36,... | collective-permute-start | bytes 1769480 | tf_op jit(solution)/shard_map/ppermute | solution.py:198
  38.9 29.4 %all-to-all-start.1 = ((bf16[8,24,1536]{2,1,0:T(8,128)(2,1)}), bf16[8,24,1536]{2,1,0:T(8,128)(2,1)S(1)}, u32[]{:S(2)}, u32[]{:S(2)}) async-start(bf16[8,24,1536]{2,1,0:T(8,128)(2,1)} %get-tuple-element.31), calls=%async_computation.1 | async-start | bytes 1179648 | tf_op jit(solution)/shard_map/all_to_all | solution.py:213
  58.0 51.7 %all-gather.4.cloned.1.call-start = ((), (), s32[]{:S(2)}) async-start(), calls=%async_computation.6 | async-start | bytes 2048000 | tf_op jit(solution)/shard_map/all_gather | solution.py:212
  69.9 39.8 %all-to-all-start.2 = ((bf16[4,192,1536]{2,1,0:T(8,128)(2,1)}), bf16[4,192,1536]{2,1,0:T(8,128)(2,1)S(1)}, u32[]{:S(2)}, u32[]{:S(2)}) async-start(bf16[4,192,1536]{2,1,0:T(8,128)(2,1)} %broadcast_in_dim.8), calls=%async_computation.2 | async-start | bytes 4718592 | tf_op jit(solution)/shard_map/all_to_all | solution.py:214
  73.9 119.1 %all-gather.6.cloned.1.call-start = ((), (), s32[]{:S(2)}) async-start(), calls=%async_computation.7 | async-start | bytes 5308416 | tf_op jit(solution)/shard_map/all_gather | solution.py:231
  109.7 6.7 %copy-start.1 = (bf16[4,192,1536]{2,1,0:T(8,128)(2,1)}, bf16[4,192,1536]{2,1,0:T(8,128)(2,1)S(1)}, u32[]{:S(2)}) copy-start(bf16[4,192,1536]{2,1,0:T(8,128)(2,1)S(1)} %all-to-all-done.2.wa_ref) | copy-start | bytes 7077892
  109.7 6.7 %collective-permute-start.2 = (bf16[4,192,1536]{2,1,0:T(8,128)(2,1)S(1)}, bf16[4,192,1536]{2,1,0:T(8,128)(2,1)S(1)}, u32[]{:S(2)}, u32[]{:S(2)}) collective-permute-start(bf16[4,192,1536]{2,1,0:T(8,128)(2,1)S(1)} %all-to-all-done.2.wa_ref), channel_id=1, source_target_pairs={{0,1},{1,0},{2,3},{3,2},{4,5},{5,4},{6,7},{7,6},{8,9},{9,8},{10,11... | collective-permute-start | bytes 7077896 | tf_op jit(solution)/shard_map/ppermute | solution.py:216
  112.3 12.5 %collective-permute-start.3 = (bf16[576,512]{1,0:T(8,128)(2,1)S(1)}, bf16[576,512]{1,0:T(8,128)(2,1)S(1)}, u32[]{:S(2)}, u32[]{:S(2)}) collective-permute-start(bf16[576,512]{1,0:T(8,128)(2,1)S(1)} %collective-permute-done), channel_id=1, source_target_pairs={{24,16},{32,40},{25,17},{33,41},{26,18},{34,42},{27,19},{35,43},{2... | collective-permute-start | bytes 1769480 | tf_op jit(solution)/shard_map/ppermute | solution.py:198
  113.0 16.8 %collective-permute-start.4 = (bf16[576,512]{1,0:T(8,128)(2,1)S(1)}, bf16[576,512]{1,0:T(8,128)(2,1)S(1)}, u32[]{:S(2)}, u32[]{:S(2)}) collective-permute-start(bf16[576,512]{1,0:T(8,128)(2,1)S(1)} %collective-permute-done.1), channel_id=1, source_target_pairs={{8,0},{48,56},{9,1},{49,57},{10,2},{50,58},{11,3},{51,59},{12,4},{... | collective-permute-start | bytes 1769480 | tf_op jit(solution)/shard_map/ppermute | solution.py:198
  124.8 6.1 %copy-start.3 = (bf16[8,80,1536]{2,1,0:T(8,128)(2,1)S(1)}, bf16[8,80,1536]{2,1,0:T(8,128)(2,1)}, u32[]{:S(2)}) copy-start(bf16[8,80,1536]{2,1,0:T(8,128)(2,1)} %get-tuple-element.38) | copy-start | bytes 5898244
  167.6 50.9 %all-to-all-start.4 = ((bf16[32,16,1536]{2,1,0:T(8,128)(2,1)}), bf16[32,16,1536]{2,1,0:T(8,128)(2,1)S(1)}, u32[]{:S(2)}, u32[]{:S(2)}) async-start(bf16[32,16,1536]{2,1,0:T(8,128)(2,1)} %bitcast.13), calls=%async_computation.4 | async-start | bytes 3145728 | tf_op jit(solution)/shard_map/all_to_all | solution.py:249
  193.0 25.0 %copy-start.11 = (f32[1536]{0:T(1024)S(1)}, f32[1536]{0:T(1024)}, u32[]{:S(2)}) copy-start(f32[1536]{0:T(1024)} %param.14) | copy-start | bytes 18436
  197.1 11.5 %collective-permute-start.10 = (bf16[16,1536]{1,0:T(8,128)(2,1)}, bf16[16,1536]{1,0:T(8,128)(2,1)S(1)}, u32[]{:S(2)}, u32[]{:S(2)}) collective-permute-start(bf16[16,1536]{1,0:T(8,128)(2,1)} %get-tuple-element.49), channel_id=1, source_target_pairs={{0,6},{1,7},{2,0},{3,1},{4,2},{5,3},{6,4},{7,5},{8,14},{9,15},{10,... | collective-permute-start | bytes 147464 | tf_op jit(solution)/shard_map/ppermute | solution.py:265
  201.4 10.8 %collective-permute-start.11 = (bf16[16,1536]{1,0:T(8,128)(2,1)}, bf16[16,1536]{1,0:T(8,128)(2,1)S(1)}, u32[]{:S(2)}, u32[]{:S(2)}) collective-permute-start(bf16[16,1536]{1,0:T(8,128)(2,1)} %get-tuple-element.50), channel_id=1, source_target_pairs={{0,7},{1,0},{2,1},{3,2},{4,3},{5,4},{6,5},{7,6},{8,15},{9,8},{10,9... | collective-permute-start | bytes 147464 | tf_op jit(solution)/shard_map/ppermute | solution.py:265
  202.4 16.2 %collective-permute-start.5 = (bf16[16,1536]{1,0:T(8,128)(2,1)}, bf16[16,1536]{1,0:T(8,128)(2,1)S(1)}, u32[]{:S(2)}, u32[]{:S(2)}) collective-permute-start(bf16[16,1536]{1,0:T(8,128)(2,1)} %get-tuple-element.44), channel_id=1, source_target_pairs={{0,1},{1,2},{2,3},{3,4},{4,5},{5,6},{6,7},{7,0},{8,9},{9,10},{10,1... | collective-permute-start | bytes 147464 | tf_op jit(solution)/shard_map/ppermute | solution.py:265
  203.2 15.4 %collective-permute-start.6 = (bf16[16,1536]{1,0:T(8,128)(2,1)}, bf16[16,1536]{1,0:T(8,128)(2,1)S(1)}, u32[]{:S(2)}, u32[]{:S(2)}) collective-permute-start(bf16[16,1536]{1,0:T(8,128)(2,1)} %get-tuple-element.45), channel_id=1, source_target_pairs={{0,2},{1,3},{2,4},{3,5},{4,6},{5,7},{6,0},{7,1},{8,10},{9,11},{10,... | collective-permute-start | bytes 147464 | tf_op jit(solution)/shard_map/ppermute | solution.py:265
  205.1 13.5 %collective-permute-start.7 = (bf16[16,1536]{1,0:T(8,128)(2,1)}, bf16[16,1536]{1,0:T(8,128)(2,1)S(1)}, u32[]{:S(2)}, u32[]{:S(2)}) collective-permute-start(bf16[16,1536]{1,0:T(8,128)(2,1)} %get-tuple-element.46), channel_id=1, source_target_pairs={{0,3},{1,4},{2,5},{3,6},{4,7},{5,0},{6,1},{7,2},{8,11},{9,12},{10,... | collective-permute-start | bytes 147464 | tf_op jit(solution)/shard_map/ppermute | solution.py:265
  208.7 10.7 %copy-start.4 = (bf16[16,1536]{1,0:T(8,128)(2,1)}, bf16[16,1536]{1,0:T(8,128)(2,1)S(1)}, u32[]{:S(2)}) copy-start(bf16[16,1536]{1,0:T(8,128)(2,1)S(1)} %collective-permute-done.10.refs_6_) | copy-start | bytes 147460
  208.7 9.9 %collective-permute-start.8 = (bf16[16,1536]{1,0:T(8,128)(2,1)}, bf16[16,1536]{1,0:T(8,128)(2,1)S(1)}, u32[]{:S(2)}, u32[]{:S(2)}) collective-permute-start(bf16[16,1536]{1,0:T(8,128)(2,1)} %get-tuple-element.47), channel_id=1, source_target_pairs={{0,4},{1,5},{2,6},{3,7},{4,0},{5,1},{6,2},{7,3},{8,12},{9,13},{10,... | collective-permute-start | bytes 147464 | tf_op jit(solution)/shard_map/ppermute | solution.py:265
  212.2 7.1 %copy-start.5 = (bf16[16,1536]{1,0:T(8,128)(2,1)}, bf16[16,1536]{1,0:T(8,128)(2,1)S(1)}, u32[]{:S(2)}) copy-start(bf16[16,1536]{1,0:T(8,128)(2,1)S(1)} %collective-permute-done.11.refs_7_) | copy-start | bytes 147460
  212.2 7.1 %collective-permute-start.9 = (bf16[16,1536]{1,0:T(8,128)(2,1)}, bf16[16,1536]{1,0:T(8,128)(2,1)S(1)}, u32[]{:S(2)}, u32[]{:S(2)}) collective-permute-start(bf16[16,1536]{1,0:T(8,128)(2,1)} %get-tuple-element.48), channel_id=1, source_target_pairs={{0,5},{1,6},{2,7},{3,0},{4,1},{5,2},{6,3},{7,4},{8,13},{9,14},{10,... | collective-permute-start | bytes 147464 | tf_op jit(solution)/shard_map/ppermute | solution.py:265
  (6 other events, 5.2 us)
Sparse Core Ops, SparseCore 0:
  60.9 48.7 all-gather.3
  131.0 61.9 all-gather.5
where the time goes:
time: 249 us; the launch traced here: 247 us
  waiting for transfers between devices  84.6 us (34%)
  starting transfers between devices  64.8 us (26%)
  blocking collectives  46.4 us (19%)
  Pallas kernels  27.1 us (11%)
  between operations  13.6 us (5%)
  local copies, waits for them, and re-layouts  9.21 us (4%)
    all_gather x1, waiting for transfers between devices, per_device(): tokens = lax.all_gather(tokens, 'y', axis=0, tiled=True)  35.8 us
    all_to_all x1, blocking collectives, per_device(): received = lax.all_to_all(send, ('x', 'c'), 0, 0, tiled=True)  30.2 us
    ppermute x7, starting transfers between devices, per_device(): lax.ppermute(far[k], ('x', 'c'), [(i, (i + k) % 8) for i in range(8)])  19.3 us
    all_to_all x1, starting transfers between devices, per_device(): w_y = lax.all_to_all(w_y, ('h', 'y'), 0, 0, tiled=True)  19.1 us
    all_gather x1, waiting for transfers between devices, per_device(): far_weights = lax.all_gather(far_piece, 'tp', axis=0, tiled=False)  19 us
    all_to_all x1, blocking collectives, per_device(): return lax.all_to_all(finished, 'tp', 0, 0, tiled=True).reshape(512, 192)  16.2 us
    all_to_all x1, waiting for transfers between devices, per_device(): got = lax.all_to_all(send, 'tp', 0, 0, tiled=True)  12.8 us
    all_to_all x1, starting transfers between devices, per_device(): got = lax.all_to_all(send, 'tp', 0, 0, tiled=True)  10 us
  transfers between devices with their start and end apart: 18, of which 7 were waited for; matrix products, arithmetic and copies ran while one was open for 3% of the time, Pallas kernels for 9%

commit v1 on v0

--- a/solution.py
+++ b/solution.py
@@ -208,7 +208,6 @@
         compiler_params=params(),
         name="unpack",
     )(keep(got), my_routes)
-    tokens, w_y, step_3 = lax.optimization_barrier((tokens, w_y, step_3))
     tokens = lax.all_gather(tokens, "y", axis=0, tiled=True)
     w_y = lax.all_to_all(w_y, ("h", "y"), 0, 0, tiled=True)
     w_x = lax.all_to_all(jnp.broadcast_to(w_y.reshape(1, 192, 1536), (4, 192, 1536)), "x", 0, 0, tiled=True)
@@ -225,7 +224,7 @@
         scratch_shapes=[pltpu.VMEM((1536, 1536), BF), pltpu.VMEM((256, 1536), F32), pltpu.VMEM((256, 1536), BF)],
         compiler_params=params(),
         name="mix",
-    )(place, tokens, w_x, w_c, gain_mix.reshape(1, 1536))
+    )(place, tokens, keep(w_x), w_c, gain_mix.reshape(1, 1536))
     step_2, step_4, _ = lax.optimization_barrier((step_2, step_4, send))
     far_piece = (step_1 + step_2) + (step_3 + step_4)
     far_weights = lax.all_gather(far_piece, "tp", axis=0, tiled=False)

time: 249 us -> 252 us (1.012)
  waiting for transfers between devices: 84.6 us -> 97.2 us
  starting transfers between devices: 64.8 us -> 55.1 us
    all_gather x1, waiting for transfers between devices: 35.8 us -> 46.8 us  [per_device(): tokens = lax.all_gather(tokens, 'y', axis=0, tiled=True)]
    all_to_all x1, starting transfers between devices: 19.1 us -> 8.47 us  [per_device(): w_y = lax.all_to_all(w_y, ('h', 'y'), 0, 0, tiled=True)]
  transfers between devices with their start and end apart: 18 -> 18, of which waited for: 7 -> 7; matrix products, arithmetic and copies ran while one was open for 3% -> 3% of each run, Pallas kernels for 9% -> 8%
where the time goes in v1:
time: 252 us; the launch traced here: 250 us
  waiting for transfers between devices  97.2 us (39%)
  starting transfers between devices  55.1 us (22%)
  blocking collectives  46.4 us (18%)
  Pallas kernels  26.3 us (10%)
  between operations  13.6 us (5%)
  local copies, waits for them, and re-layouts  9.21 us (4%)
    all_gather x1, waiting for transfers between devices, per_device(): tokens = lax.all_gather(tokens, 'y', axis=0, tiled=True)  46.8 us
    all_to_all x1, blocking collectives, per_device(): received = lax.all_to_all(send, ('x', 'c'), 0, 0, tiled=True)  30.1 us
    ppermute x7, starting transfers between devices, per_device(): lax.ppermute(far[k], ('x', 'c'), [(i, (i + k) % 8) for i in range(8)])  19.3 us
    all_gather x1, waiting for transfers between devices, per_device(): far_weights = lax.all_gather(far_piece, 'tp', axis=0, tiled=False)  19 us
    all_to_all x1, blocking collectives, per_device(): return lax.all_to_all(finished, 'tp', 0, 0, tiled=True).reshape(512, 192)  16.2 us
    all_to_all x1, waiting for transfers between devices, per_device(): got = lax.all_to_all(send, 'tp', 0, 0, tiled=True)  13.5 us
    all_to_all x1, starting transfers between devices, per_device(): got = lax.all_to_all(send, 'tp', 0, 0, tiled=True)  10 us
    all_to_all x1, waiting for transfers between devices, per_device(): w_y = lax.all_to_all(w_y, ('h', 'y'), 0, 0, tiled=True)  9.55 us
  transfers between devices with their start and end apart: 18, of which 7 were waited for; matrix products, arithmetic and copies ran while one was open for 3% of the time, Pallas kernels for 8%

profile of v1, /device:TPU:57, one launch (start us, length us, event | category | flops | bytes accessed | tf_op | source)
XLA Modules:
  0.0 249.9 jit_solution(6064895724361901504)
XLA Ops:
  6.5 2.0 pack.1
  8.5 10.0 %all-to-all-start = ((bf16[8,88,384]{2,1,0:T(8,128)(2,1)}), bf16[8,88,384]{2,1,0:T(8,128)(2,1)S(1)}, u32[]{:S(2)}, u32[]{:S(2)}) async-start(bf16[8,88,384]{2,1,0:T(8,128)(2,1)} %pack.1), calls=%async_computation | async-start | bytes 1081344 | tf_op jit(solution)/shard_map/all_to_all | solution.py:180
  19.2 2.6 %piece.1 = bf16[576,512]{1,0:T(8,128)(2,1)} custom-call(s32[6]{0:T(128)} %stack.27.place_ref, bf16[1,1536,512]{2,1,0:T(8,128)(2,1)} %wg_ref.3, bf16[1,1536,512]{2,1,0:T(8,128)(2,1)} %wu_ref.3, bf16[1,512,1536]{2,1,0:T(8,128)(2,1)} %wd_ref.3), custom_call_target="tpu_custom_call" | custom-call | tf_op jit(solution)/shard_map/piece/pallas_call | solution.py:182
  23.3 13.5 %all-to-all-done.got_ref = bf16[8,88,384]{2,1,0:T(8,128)(2,1)S(1)} async-done(((bf16[8,88,384]{2,1,0:T(8,128)(2,1)}), bf16[8,88,384]{2,1,0:T(8,128)(2,1)S(1)}, u32[]{:S(2)}, u32[]{:S(2)}) %all-to-all-start) | async-done | bytes 540704 | tf_op jit(solution)/shard_map/all_to_all | solution.py:180
  36.9 1.9 unpack.1
  38.8 8.5 %all-to-all-start.1 = ((bf16[8,24,1536]{2,1,0:T(8,128)(2,1)}), bf16[8,24,1536]{2,1,0:T(8,128)(2,1)S(1)}, u32[]{:S(2)}, u32[]{:S(2)}) async-start(bf16[8,24,1536]{2,1,0:T(8,128)(2,1)} %get-tuple-element.26), calls=%async_computation.1 | async-start | bytes 1179648 | tf_op jit(solution)/shard_map/all_to_all | solution.py:212
  48.0 9.5 %all-to-all-done.1 = bf16[8,24,1536]{2,1,0:T(8,128)(2,1)S(1)} async-done(((bf16[8,24,1536]{2,1,0:T(8,128)(2,1)}), bf16[8,24,1536]{2,1,0:T(8,128)(2,1)S(1)}, u32[]{:S(2)}, u32[]{:S(2)}) %all-to-all-start.1) | async-done | bytes 589856 | tf_op jit(solution)/shard_map/all_to_all | solution.py:212
  59.2 4.1 %all-to-all-start.2 = ((bf16[4,192,1536]{2,1,0:T(8,128)(2,1)}), bf16[4,192,1536]{2,1,0:T(8,128)(2,1)S(1)}, u32[]{:S(2)}, u32[]{:S(2)}) async-start(bf16[4,192,1536]{2,1,0:T(8,128)(2,1)} %broadcast_in_dim.8), calls=%async_computation.2 | async-start | bytes 4718592 | tf_op jit(solution)/shard_map/all_to_all | solution.py:213
  64.8 46.8 %all-gather.4.cloned.1.call-done.tok_ref = bf16[256,3200]{1,0:T(8,128)(2,1)} async-done(((bf16[64,3200]{1,0:T(8,128)(2,1)}), bf16[256,3200]{1,0:T(8,128)(2,1)}) %all-gather.4.cloned.1.call-update) | async-done | bytes 1638416 | tf_op jit(solution)/shard_map/all_gather | solution.py:211
  111.6 2.6 %collective-permute-start.2 = (bf16[4,192,1536]{2,1,0:T(8,128)(2,1)S(1)}, bf16[4,192,1536]{2,1,0:T(8,128)(2,1)S(1)}, u32[]{:S(2)}, u32[]{:S(2)}) collective-permute-start(bf16[4,192,1536]{2,1,0:T(8,128)(2,1)S(1)} %all-to-all-done.2.wa_ref), channel_id=1, source_target_pairs={{0,1},{1,0},{2,3},{3,2},{4,5},{5,4},{6,7},{7,6},{8,9},{9,8},{10,11... | collective-permute-start | bytes 7077896 | tf_op jit(solution)/shard_map/ppermute | solution.py:215
  119.8 6.2 %mix.1 = (bf16[8,80,1536]{2,1,0:T(8,128)(2,1)}, f32[64,1536]{1,0:T(8,128)}) custom-call(s32[6]{0:T(128)} %stack.27.place_ref, bf16[256,3200]{1,0:T(8,128)(2,1)} %all-gather.4.cloned.1.call-done.tok_ref, bf16[4,192,1536]{2,1,0:T(8,128)(2,1)S(1)} %all-to-all-done.2.wa_ref, bf16[4,192,1536]{2,1,0:T(8,128)(2,1)} %copy-done.1, f32[1,1536]{1,0:T(1,128)} %reshape.14.gain_ref), custom_call_target="tpu_custom_call" | custom-call | tf_op jit(solution)/shard_map/mix/pallas_call | solution.py:219
  126.0 6.0 %collective-permute-done.4 = bf16[576,512]{1,0:T(8,128)(2,1)S(1)} collective-permute-done((bf16[576,512]{1,0:T(8,128)(2,1)}, bf16[576,512]{1,0:T(8,128)(2,1)S(1)}, u32[]{:S(2)}, u32[]{:S(2)}) %collective-permute-start.4) | collective-permute-done | bytes 589856 | tf_op jit(solution)/shard_map/ppermute | solution.py:198
  132.0 2.1 add_add_fusion
  134.1 30.1 %all_to_all.30.x_ref = bf16[8,80,1536]{2,1,0:T(8,128)(2,1)} all-to-all(bf16[8,80,1536]{2,1,0:T(8,128)(2,1)S(1)} %copy-done.2), channel_id=1, replica_groups=mesh['tp'=8,'h'=2,'y'=4,'x'=4,'c'=2] {'x','c'}, dimensions={0} | all-to-all | bytes 3932160 | tf_op jit(solution)/shard_map/all_to_all | solution.py:231
  164.2 6.6 %near.1 = bf16[4,8,16,1536]{3,2,1,0:T(8,128)(2,1)} custom-call(bf16[8,80,1536]{2,1,0:T(8,128)(2,1)} %all_to_all.30.x_ref, bf16[1,1536,512]{2,1,0:T(8,128)(2,1)} %wg_ref.3, bf16[1,1536,512]{2,1,0:T(8,128)(2,1)} %wu_ref.3, bf16[1,512,1536]{2,1,0:T(8,128)(2,1)} %wd_ref.3), custom_call_target="tpu_custom_call" | custom-call | tf_op jit(solution)/shard_map/near/pallas_call | solution.py:234
  170.8 6.4 %all-to-all-start.4 = ((bf16[32,16,1536]{2,1,0:T(8,128)(2,1)}), bf16[32,16,1536]{2,1,0:T(8,128)(2,1)S(1)}, u32[]{:S(2)}, u32[]{:S(2)}) async-start(bf16[32,16,1536]{2,1,0:T(8,128)(2,1)} %bitcast.13), calls=%async_computation.4 | async-start | bytes 3145728 | tf_op jit(solution)/shard_map/all_to_all | solution.py:248
  177.2 19.0 %all-gather.6.cloned.1.call-done = bf16[4608,512]{1,0:T(8,128)(2,1)} async-done(((bf16[576,512]{1,0:T(8,128)(2,1)}), bf16[4608,512]{1,0:T(8,128)(2,1)}) %all-gather.6.cloned.1.call-update) | async-done | bytes 4718608 | tf_op jit(solution)/shard_map/all_gather | solution.py:230
  196.2 4.1 %far.1 = (bf16[16,1536]{1,0:T(8,128)(2,1)}, bf16[16,1536]{1,0:T(8,128)(2,1)}, bf16[16,1536]{1,0:T(8,128)(2,1)}, bf16[16,1536]{1,0:T(8,128)(2,1)}, bf16[16,1536]{...) custom-call(s32[6]{0:T(128)} %stack.27.place_ref, ...), custom_call_target="tpu_custom_call" | custom-call | tf_op jit(solution)/shard_map/far/pallas_call | solution.py:249
  200.3 4.3 %collective-permute-start.10 = (bf16[16,1536]{1,0:T(8,128)(2,1)}, bf16[16,1536]{1,0:T(8,128)(2,1)S(1)}, u32[]{:S(2)}, u32[]{:S(2)}) collective-permute-start(bf16[16,1536]{1,0:T(8,128)(2,1)} %get-tuple-element.43), channel_id=1, source_target_pairs={{0,6},{1,7},{2,0},{3,1},{4,2},{5,3},{6,4},{7,5},{8,14},{9,15},{10,... | collective-permute-start | bytes 147464 | tf_op jit(solution)/shard_map/ppermute | solution.py:264
  208.3 3.5 %collective-permute-start.7 = (bf16[16,1536]{1,0:T(8,128)(2,1)}, bf16[16,1536]{1,0:T(8,128)(2,1)S(1)}, u32[]{:S(2)}, u32[]{:S(2)}) collective-permute-start(bf16[16,1536]{1,0:T(8,128)(2,1)} %get-tuple-element.40), channel_id=1, source_target_pairs={{0,3},{1,4},{2,5},{3,6},{4,7},{5,0},{6,1},{7,2},{8,11},{9,12},{10,... | collective-permute-start | bytes 147464 | tf_op jit(solution)/shard_map/ppermute | solution.py:264
  211.9 3.5 %collective-permute-start.8 = (bf16[16,1536]{1,0:T(8,128)(2,1)}, bf16[16,1536]{1,0:T(8,128)(2,1)S(1)}, u32[]{:S(2)}, u32[]{:S(2)}) collective-permute-start(bf16[16,1536]{1,0:T(8,128)(2,1)} %get-tuple-element.41), channel_id=1, source_target_pairs={{0,4},{1,5},{2,6},{3,7},{4,0},{5,1},{6,2},{7,3},{8,12},{9,13},{10,... | collective-permute-start | bytes 147464 | tf_op jit(solution)/shard_map/ppermute | solution.py:264
  215.4 4.3 %collective-permute-start.9 = (bf16[16,1536]{1,0:T(8,128)(2,1)}, bf16[16,1536]{1,0:T(8,128)(2,1)S(1)}, u32[]{:S(2)}, u32[]{:S(2)}) collective-permute-start(bf16[16,1536]{1,0:T(8,128)(2,1)} %get-tuple-element.42), channel_id=1, source_target_pairs={{0,5},{1,6},{2,7},{3,0},{4,1},{5,2},{6,3},{7,4},{8,13},{9,14},{10,... | collective-permute-start | bytes 147464 | tf_op jit(solution)/shard_map/ppermute | solution.py:264
  223.1 2.9 %close.1 = bf16[8,64,192]{2,1,0:T(8,128)(2,1)} custom-call(s32[6]{0:T(128)} %stack.27.place_ref, s32[64,8]{1,0:T(8,128)} %copy.14.routes_ref, f32[64,8]{1,0:T(8,128)} %copy.15.gates_ref, f32[64,1536]{1,0:T(8,128)} %get-tuple-element.31.hid_ref, f32[1,1536]{1,0:T(1,128)} %reshape.15.gain_ref, bf16[32,16,1536]{2,1,0:T(8,128)(2,1)S(1)} %all-to-all-done.4.near_ref, ...), custom_call_target="tpu_custom_call" | custom-call | tf_op jit(solution)/shard_map/close/pallas_call | solution.py:266
  226.0 16.2 %all_to_all.31 = bf16[8,64,192]{2,1,0:T(8,128)(2,1)S(1)} all-to-all(bf16[8,64,192]{2,1,0:T(8,128)(2,1)} %close.1), channel_id=1, replica_groups=mesh['tp'=8,'h'=2,'y'=4,'x'=4,'c'=2] {'tp'}, dimensions={0} | all-to-all | bytes 393216 | tf_op jit(solution)/shard_map/all_to_all | solution.py:274
  (57 shorter events, 19.4 us)
Async XLA Ops:
  6.5 16.0 %copy-start = (s32[512,8]{0,1:T(8,128)S(1)}, s32[512,8]{0,1:T(8,128)}, u32[]{:S(2)}) copy-start(s32[512,8]{0,1:T(8,128)} %param.15) | copy-start | bytes 49156
  8.5 28.3 %all-to-all-start = ((bf16[8,88,384]{2,1,0:T(8,128)(2,1)}), bf16[8,88,384]{2,1,0:T(8,128)(2,1)S(1)}, u32[]{:S(2)}, u32[]{:S(2)}) async-start(bf16[8,88,384]{2,1,0:T(8,128)(2,1)} %pack.1), calls=%async_computation | async-start | bytes 1081344 | tf_op jit(solution)/shard_map/all_to_all | solution.py:180
  21.8 1.5 collective-permute-start
  38.8 18.7 %all-to-all-start.1 = ((bf16[8,24,1536]{2,1,0:T(8,128)(2,1)}), bf16[8,24,1536]{2,1,0:T(8,128)(2,1)S(1)}, u32[]{:S(2)}, u32[]{:S(2)}) async-start(bf16[8,24,1536]{2,1,0:T(8,128)(2,1)} %get-tuple-element.26), calls=%async_computation.1 | async-start | bytes 1179648 | tf_op jit(solution)/shard_map/all_to_all | solution.py:212
  47.3 64.4 %all-gather.4.cloned.1.call-start = ((), (), s32[]{:S(2)}) async-start(), calls=%async_computation.6 | async-start | bytes 2048000 | tf_op jit(solution)/shard_map/all_gather | solution.py:211
  59.2 4.2 %copy-start.3 = (bf16[576,512]{1,0:T(8,128)(2,1)S(1)}, bf16[576,512]{1,0:T(8,128)(2,1)}, u32[]{:S(2)}) copy-start(bf16[576,512]{1,0:T(8,128)(2,1)} %piece.1) | copy-start | bytes 1769476
  59.2 52.5 %all-to-all-start.2 = ((bf16[4,192,1536]{2,1,0:T(8,128)(2,1)}), bf16[4,192,1536]{2,1,0:T(8,128)(2,1)S(1)}, u32[]{:S(2)}, u32[]{:S(2)}) async-start(bf16[4,192,1536]{2,1,0:T(8,128)(2,1)} %broadcast_in_dim.8), calls=%async_computation.2 | async-start | bytes 4718592 | tf_op jit(solution)/shard_map/all_to_all | solution.py:213
  63.3 132.9 %all-gather.6.cloned.1.call-start = ((), (), s32[]{:S(2)}) async-start(), calls=%async_computation.7 | async-start | bytes 5308416 | tf_op jit(solution)/shard_map/all_gather | solution.py:230
  63.3 1.5 collective-permute-start.1
  111.6 6.7 %collective-permute-start.2 = (bf16[4,192,1536]{2,1,0:T(8,128)(2,1)S(1)}, bf16[4,192,1536]{2,1,0:T(8,128)(2,1)S(1)}, u32[]{:S(2)}, u32[]{:S(2)}) collective-permute-start(bf16[4,192,1536]{2,1,0:T(8,128)(2,1)S(1)} %all-to-all-done.2.wa_ref), channel_id=1, source_target_pairs={{0,1},{1,0},{2,3},{3,2},{4,5},{5,4},{6,7},{7,6},{8,9},{9,8},{10,11... | collective-permute-start | bytes 7077896 | tf_op jit(solution)/shard_map/ppermute | solution.py:215
  114.2 11.7 %collective-permute-start.3 = (bf16[576,512]{1,0:T(8,128)(2,1)S(1)}, bf16[576,512]{1,0:T(8,128)(2,1)S(1)}, u32[]{:S(2)}, u32[]{:S(2)}) collective-permute-start(bf16[576,512]{1,0:T(8,128)(2,1)S(1)} %collective-permute-done), channel_id=1, source_target_pairs={{24,16},{32,40},{25,17},{33,41},{26,18},{34,42},{27,19},{35,43},{2... | collective-permute-start | bytes 1769480 | tf_op jit(solution)/shard_map/ppermute | solution.py:198
  114.9 17.1 %collective-permute-start.4 = (bf16[576,512]{1,0:T(8,128)(2,1)}, bf16[576,512]{1,0:T(8,128)(2,1)S(1)}, u32[]{:S(2)}, u32[]{:S(2)}) collective-permute-start(bf16[576,512]{1,0:T(8,128)(2,1)} %collective-permute-done.1), channel_id=1, source_target_pairs={{8,0},{48,56},{9,1},{49,57},{10,2},{50,58},{11,3},{51,59},{12,4},{... | collective-permute-start | bytes 1769480 | tf_op jit(solution)/shard_map/ppermute | solution.py:198
  125.9 8.1 %copy-start.2 = (bf16[8,80,1536]{2,1,0:T(8,128)(2,1)S(1)}, bf16[8,80,1536]{2,1,0:T(8,128)(2,1)}, u32[]{:S(2)}) copy-start(bf16[8,80,1536]{2,1,0:T(8,128)(2,1)} %get-tuple-element.32) | copy-start | bytes 5898244
  170.8 50.9 %all-to-all-start.4 = ((bf16[32,16,1536]{2,1,0:T(8,128)(2,1)}), bf16[32,16,1536]{2,1,0:T(8,128)(2,1)S(1)}, u32[]{:S(2)}, u32[]{:S(2)}) async-start(bf16[32,16,1536]{2,1,0:T(8,128)(2,1)} %bitcast.13), calls=%async_computation.4 | async-start | bytes 3145728 | tf_op jit(solution)/shard_map/all_to_all | solution.py:248
  196.2 25.0 %copy-start.11 = (f32[1536]{0:T(1024)S(1)}, f32[1536]{0:T(1024)}, u32[]{:S(2)}) copy-start(f32[1536]{0:T(1024)} %param.14) | copy-start | bytes 18436
  200.3 11.5 %collective-permute-start.10 = (bf16[16,1536]{1,0:T(8,128)(2,1)}, bf16[16,1536]{1,0:T(8,128)(2,1)S(1)}, u32[]{:S(2)}, u32[]{:S(2)}) collective-permute-start(bf16[16,1536]{1,0:T(8,128)(2,1)} %get-tuple-element.43), channel_id=1, source_target_pairs={{0,6},{1,7},{2,0},{3,1},{4,2},{5,3},{6,4},{7,5},{8,14},{9,15},{10,... | collective-permute-start | bytes 147464 | tf_op jit(solution)/shard_map/ppermute | solution.py:264
  204.6 10.8 %collective-permute-start.11 = (bf16[16,1536]{1,0:T(8,128)(2,1)}, bf16[16,1536]{1,0:T(8,128)(2,1)S(1)}, u32[]{:S(2)}, u32[]{:S(2)}) collective-permute-start(bf16[16,1536]{1,0:T(8,128)(2,1)} %get-tuple-element.44), channel_id=1, source_target_pairs={{0,7},{1,0},{2,1},{3,2},{4,3},{5,4},{6,5},{7,6},{8,15},{9,8},{10,9... | collective-permute-start | bytes 147464 | tf_op jit(solution)/shard_map/ppermute | solution.py:264
  205.6 16.2 %collective-permute-start.5 = (bf16[16,1536]{1,0:T(8,128)(2,1)}, bf16[16,1536]{1,0:T(8,128)(2,1)S(1)}, u32[]{:S(2)}, u32[]{:S(2)}) collective-permute-start(bf16[16,1536]{1,0:T(8,128)(2,1)} %get-tuple-element.38), channel_id=1, source_target_pairs={{0,1},{1,2},{2,3},{3,4},{4,5},{5,6},{6,7},{7,0},{8,9},{9,10},{10,1... | collective-permute-start | bytes 147464 | tf_op jit(solution)/shard_map/ppermute | solution.py:264
  206.4 15.4 %collective-permute-start.6 = (bf16[16,1536]{1,0:T(8,128)(2,1)}, bf16[16,1536]{1,0:T(8,128)(2,1)S(1)}, u32[]{:S(2)}, u32[]{:S(2)}) collective-permute-start(bf16[16,1536]{1,0:T(8,128)(2,1)} %get-tuple-element.39), channel_id=1, source_target_pairs={{0,2},{1,3},{2,4},{3,5},{4,6},{5,7},{6,0},{7,1},{8,10},{9,11},{10,... | collective-permute-start | bytes 147464 | tf_op jit(solution)/shard_map/ppermute | solution.py:264
  208.3 13.5 %collective-permute-start.7 = (bf16[16,1536]{1,0:T(8,128)(2,1)}, bf16[16,1536]{1,0:T(8,128)(2,1)S(1)}, u32[]{:S(2)}, u32[]{:S(2)}) collective-permute-start(bf16[16,1536]{1,0:T(8,128)(2,1)} %get-tuple-element.40), channel_id=1, source_target_pairs={{0,3},{1,4},{2,5},{3,6},{4,7},{5,0},{6,1},{7,2},{8,11},{9,12},{10,... | collective-permute-start | bytes 147464 | tf_op jit(solution)/shard_map/ppermute | solution.py:264
  211.8 10.7 %copy-start.4 = (bf16[16,1536]{1,0:T(8,128)(2,1)}, bf16[16,1536]{1,0:T(8,128)(2,1)S(1)}, u32[]{:S(2)}) copy-start(bf16[16,1536]{1,0:T(8,128)(2,1)S(1)} %collective-permute-done.10.refs_6_) | copy-start | bytes 147460
  211.9 9.9 %collective-permute-start.8 = (bf16[16,1536]{1,0:T(8,128)(2,1)}, bf16[16,1536]{1,0:T(8,128)(2,1)S(1)}, u32[]{:S(2)}, u32[]{:S(2)}) collective-permute-start(bf16[16,1536]{1,0:T(8,128)(2,1)} %get-tuple-element.41), channel_id=1, source_target_pairs={{0,4},{1,5},{2,6},{3,7},{4,0},{5,1},{6,2},{7,3},{8,12},{9,13},{10,... | collective-permute-start | bytes 147464 | tf_op jit(solution)/shard_map/ppermute | solution.py:264
  215.4 7.1 %copy-start.5 = (bf16[16,1536]{1,0:T(8,128)(2,1)}, bf16[16,1536]{1,0:T(8,128)(2,1)S(1)}, u32[]{:S(2)}) copy-start(bf16[16,1536]{1,0:T(8,128)(2,1)S(1)} %collective-permute-done.11.refs_7_) | copy-start | bytes 147460
  215.4 7.1 %collective-permute-start.9 = (bf16[16,1536]{1,0:T(8,128)(2,1)}, bf16[16,1536]{1,0:T(8,128)(2,1)S(1)}, u32[]{:S(2)}, u32[]{:S(2)}) collective-permute-start(bf16[16,1536]{1,0:T(8,128)(2,1)} %get-tuple-element.42), channel_id=1, source_target_pairs={{0,5},{1,6},{2,7},{3,0},{4,1},{5,2},{6,3},{7,4},{8,13},{9,14},{10,... | collective-permute-start | bytes 147464 | tf_op jit(solution)/shard_map/ppermute | solution.py:264
  (6 other events, 5.1 us)
Sparse Core Ops, SparseCore 0:
  50.2 61.3 all-gather.3
  134.2 61.9 all-gather.5
